TPU v7x, 512 devices: a whole 4x8x8 slice. The times are simulated.
512 devices in a mesh: row: 32 (over x, y), col: 16 (over z, core).
Axes of the slice: x: 4, y: 8, z: 8, core: 2. Of those that a mesh axis runs over, the one named last changes fastest.
Arguments:
- kernel: float32 [1, 8192, 2, 4096], P(None, 'row', None, 'col'), may hold values from 0 to 1.5, as said below
Outputs:
- factored: float32 [1, 8192, 2, 4096], P(None, 'row', None, 'col')
Inputs may be any that keep to these rules, and one draw needn't show every extreme that they name: kernel is symmetric and positive definite with all eigenvalues at least about 0.5 (up to float32 rounding of the draw); its entries lie between 0 and 1.5.
All inputs are finite; a program needn't handle non-finite values.
Results may differ from a plain program's by a relative error of at most 0.0003.
Values sent between devices are 32-bit elements; how exact they have to be, the bound alone decides.
A program may use at most 64 MiB of HBM per device.

v0:
```python
import jax
import jax.numpy as jnp
from jax import lax
from jax.sharding import PartitionSpec as P

PANELS = 3


def broadcast(value, axis, source):
    kept = jnp.where(lax.axis_index(axis) == source, value, 0).astype(value.dtype)
    return lax.psum(kept, axis)


def solve_rows(factor, blocks):
    count, height, width = blocks.shape
    flat = blocks.reshape(count * height, factor.shape[0])
    solved = lax.linalg.triangular_solve(
        factor, flat, left_side=False, lower=True, transpose_a=True
    )
    return solved.reshape(count, height, factor.shape[0])


def keep_after(blocks, block_ids, step):
    return jnp.where((block_ids > step)[:, None, None], blocks, jnp.float32(0.0))


def subtract(target, rows_here, cols_here):
    return target - jnp.einsum(
        "aik,bjk->aibj", rows_here, cols_here, precision=lax.Precision.HIGHEST
    )


def apply_update(matrix, rows_here, cols_here):
    return subtract(matrix, rows_here, cols_here)


def shards(kernel):
    blocks_r, width, blocks_c, _ = kernel.shape
    n_row = lax.axis_size("row")
    n_col = lax.axis_size("col")
    ratio = n_row // n_col
    row_pos = lax.axis_index("row")
    col_pos = lax.axis_index("col")
    row_ids = jnp.arange(blocks_r, dtype=jnp.int32) * n_row + row_pos
    col_ids = jnp.arange(blocks_c, dtype=jnp.int32) * n_col + col_pos
    identity = jnp.eye(width, dtype=jnp.float32)
    matrix = kernel
    for step in range(PANELS):
        corner = broadcast(matrix[0, :, 0, :], "row", step)
        corner = jnp.where(col_pos == step, corner, identity)
        factor = jnp.linalg.cholesky(corner)
        solved = solve_rows(factor, matrix[:, :, 0, :])
        rows_here = broadcast(keep_after(solved, row_ids, step), "col", step)
        pieces = []
        for member in range(ratio):
            pieces.append(broadcast(rows_here, "row", col_pos + member * n_col))
        cols_here = jnp.stack(pieces, axis=1).reshape(blocks_c, width, width)
        matrix = apply_update(matrix, rows_here, cols_here)
        ids = row_ids[:, None, None]
        new_panel = jnp.where(
            ids < step, jnp.float32(0.0), jnp.where(ids == step, factor[None, :, :], solved)
        )
        column = jnp.where(col_pos == step, new_panel, matrix[:, :, 0, :])
        matrix = matrix.at[:, :, 0, :].set(column)
    upper = (row_ids < PANELS)[:, None, None, None] & (col_ids >= PANELS)[None, None, :, None]
    return jnp.where(upper, jnp.float32(0.0), matrix)


def solution(mesh):
    in_specs = (P(None, "row", None, "col"),)
    out_specs = P(None, "row", None, "col")
    return jax.shard_map(shards, mesh=mesh, in_specs=in_specs, out_specs=out_specs, check_vma=False)
```

profile of v0, /device:TPU:64, one launch (start us, length us, event | category | flops | bytes accessed | tf_op | source)
XLA Modules:
  0.0 1505.2 jit_solution(10996868907144905273)
XLA Ops:
  6.5 1.2 copy.11
  7.8 0.7 broadcast_select_fusion.3
  8.6 161.3 %all-reduce.14.cloned.1.call-done = f32[256,256]{0,1:T(8,128)} async-done(((f32[256,256]{0,1:T(8,128)}), f32[256,256]{0,1:T(8,128)}) %all-reduce.14.cloned.1.call-update) | async-done | bytes 262160 | tf_op jit(solution)/shard_map/psum | solution.py:11
  170.1 0.8 copy-done.3
  170.9 11.7 cholesky.172
  182.8 9.8 custom-call.15
  193.2 11.7 cholesky.189
  205.1 0.7 compare_reduce_fusion.4
  207.3 4.5 while.9
  207.5 0.6 fusion.68
  208.1 1.4 dynamic-slice.44
  209.6 0.6 fusion.68
  210.2 1.4 dynamic-slice.44
  211.8 19.7 %custom-call.16 = f32[2,128,128]{1,2,0:T(8,128)S(1)} custom-call(f32[2,128,128]{2,1,0:T(8,128)S(1)} %get-tuple-element.63), custom_call_target="InvertDiagBlocksLowerTriangular" | custom-call | tf_op jit(solution)/shard_map/triangular_solve/custom-call.0 | solution.py:17
  232.1 0.3 fusion.38
  232.4 0.7 select_bitcast_fusion.8
  233.3 109.4 %all-reduce.16.cloned.1.call-done = f32[1,256,256]{1,2,0:T(8,128)} async-done(((f32[1,256,256]{1,2,0:T(8,128)}), f32[1,256,256]{1,2,0:T(8,128)}) %all-reduce.16.cloned.1.call-update) | async-done | bytes 262160 | tf_op jit(solution)/shard_map/psum | solution.py:11
  342.6 1.8 select_bitcast_fusion.7
  344.5 162.8 %all-reduce.30.cloned.1.call-done = (f32[1,1,256,256]{2,3,1,0:T(8,128)}, f32[1,1,256,256]{2,3,1,0:T(8,128)}) async-done(((f32[1,1,256,256]{2,3,1,0:T(8,128)}, f32[1,1,256,256]{2,3,1,0:T(8,128)}), (f32[1,1,256,256]{2,3,1,0:T(8,128)}, f32[1,1,256,256]{2,3,1,0:T(8,128)})) %all-reduce.30.cloned.1.call-update) | async-done | bytes 524304 | tf_op jit(solution)/shard_map/psum | solution.py:11
  507.3 2.0 fusion
  509.4 0.8 broadcast_select_fusion.2
  510.2 152.8 %all-reduce.18.cloned.1.call-done = f32[256,256]{0,1:T(8,128)} async-done(((f32[256,256]{0,1:T(8,128)}), f32[256,256]{0,1:T(8,128)}) %all-reduce.18.cloned.1.call-update) | async-done | bytes 262160 | tf_op jit(solution)/shard_map/psum | solution.py:11
  663.2 0.8 copy-done.4
  664.0 11.7 cholesky.206
  675.9 9.8 custom-call.17
  686.3 11.7 cholesky.223
  698.1 0.6 compare_reduce_fusion.3
  698.8 0.7 compare_reduce_fusion.2
  700.9 4.6 while.10
  701.2 0.6 fusion.69
  701.8 1.4 dynamic-slice.46
  703.4 0.6 fusion.69
  703.9 1.4 dynamic-slice.46
  705.5 19.7 %custom-call.18 = f32[2,128,128]{1,2,0:T(8,128)S(1)} custom-call(f32[2,128,128]{2,1,0:T(8,128)S(1)} %get-tuple-element.64), custom_call_target="InvertDiagBlocksLowerTriangular" | custom-call | tf_op jit(solution)/shard_map/triangular_solve/custom-call.0 | solution.py:17
  725.5 0.3 convolution_subtract_fusion.1
  725.8 0.3 fusion.34
  726.2 0.7 select_bitcast_fusion.5
  727.0 109.6 %all-reduce.20.cloned.1.call-done = f32[1,256,256]{1,2,0:T(8,128)} async-done(((f32[1,256,256]{1,2,0:T(8,128)}), f32[1,256,256]{1,2,0:T(8,128)}) %all-reduce.20.cloned.1.call-update) | async-done | bytes 262160 | tf_op jit(solution)/shard_map/psum | solution.py:11
  836.6 1.8 select_bitcast_fusion.4
  838.5 162.6 %all-reduce.28.cloned.1.call-done = (f32[1,1,256,256]{2,3,1,0:T(8,128)}, f32[1,1,256,256]{2,3,1,0:T(8,128)}) async-done(((f32[1,1,256,256]{2,3,1,0:T(8,128)}, f32[1,1,256,256]{2,3,1,0:T(8,128)}), (f32[1,1,256,256]{2,3,1,0:T(8,128)}, f32[1,1,256,256]{2,3,1,0:T(8,128)})) %all-reduce.28.cloned.1.call-update) | async-done | bytes 524304 | tf_op jit(solution)/shard_map/psum | solution.py:11
  1001.1 2.0 fusion.1
  1003.1 0.8 broadcast_select_fusion.1
  1004.0 152.9 %all-reduce.22.cloned.1.call-done = f32[256,256]{0,1:T(8,128)} async-done(((f32[256,256]{0,1:T(8,128)}), f32[256,256]{0,1:T(8,128)}) %all-reduce.22.cloned.1.call-update) | async-done | bytes 262160 | tf_op jit(solution)/shard_map/psum | solution.py:11
  1156.9 1.0 convert_select_fusion
  1158.0 0.8 copy-done.5
  1158.9 11.7 cholesky.240
  1170.7 9.8 custom-call.19
  1181.1 11.7 cholesky.257
  1193.0 0.6 compare_reduce_fusion.1
  1193.6 0.7 compare_reduce_fusion
  1195.8 4.6 while.11
  1196.1 0.6 fusion.70
  1196.7 1.4 dynamic-slice.48
  1198.2 0.6 fusion.70
  1198.8 1.4 dynamic-slice.48
  1200.4 19.7 %custom-call.20 = f32[2,128,128]{1,2,0:T(8,128)S(1)} custom-call(f32[2,128,128]{2,1,0:T(8,128)S(1)} %get-tuple-element.65), custom_call_target="InvertDiagBlocksLowerTriangular" | custom-call | tf_op jit(solution)/shard_map/triangular_solve/custom-call.0 | solution.py:17
  1220.4 0.3 convolution_subtract_fusion
  1220.7 0.3 fusion.30
  1221.0 0.7 select_bitcast_fusion.2
  1221.8 108.5 %all-reduce.24.cloned.1.call-done = f32[1,256,256]{1,2,0:T(8,128)} async-done(((f32[1,256,256]{1,2,0:T(8,128)}), f32[1,256,256]{1,2,0:T(8,128)}) %all-reduce.24.cloned.1.call-update) | async-done | bytes 262160 | tf_op jit(solution)/shard_map/psum | solution.py:11
  1330.3 1.8 select_bitcast_fusion.1
  1332.2 162.8 %all-reduce.26.cloned.1.call-done = (f32[1,1,256,256]{2,3,1,0:T(8,128)}, f32[1,1,256,256]{2,3,1,0:T(8,128)}) async-done(((f32[1,1,256,256]{2,3,1,0:T(8,128)}, f32[1,1,256,256]{2,3,1,0:T(8,128)}), (f32[1,1,256,256]{2,3,1,0:T(8,128)}, f32[1,1,256,256]{2,3,1,0:T(8,128)})) %all-reduce.26.cloned.1.call-update) | async-done | bytes 524304 | tf_op jit(solution)/shard_map/psum | solution.py:11
  1495.0 2.0 fusion.2
  1497.2 1.0 copy.28
  (104 shorter events, 6.0 us)
Async XLA Ops:
  6.5 163.4 %all-reduce.14.cloned.1.call-start = ((), (), s32[]{:S(2)}) async-start(), calls=%async_computation | async-start | bytes 524288 | tf_op jit(solution)/shard_map/psum | solution.py:11
  8.5 334.1 %all-reduce.16.cloned.1.call-start = ((), (), s32[]{:S(2)}) async-start(), calls=%async_computation.1 | async-start | bytes 524288 | tf_op jit(solution)/shard_map/psum | solution.py:11
  169.9 1.0 copy-start.3
  233.2 274.1 %all-reduce.30.cloned.1.call-start = ((), (), s32[]{:S(2)}) async-start(), calls=%async_computation.8 | async-start | bytes 1048576 | tf_op jit(solution)/shard_map/psum | solution.py:11
  344.4 162.9 %copy-start.1 = (f32[1,256,256]{1,2,0:T(8,128)S(1)}, f32[1,256,256]{1,2,0:T(8,128)}, u32[]{:S(2)}) copy-start(f32[1,256,256]{1,2,0:T(8,128)} %all-reduce.16.cloned.1.call-done) | copy-start | bytes 786436
  344.4 318.6 %all-reduce.18.cloned.1.call-start = ((), (), s32[]{:S(2)}) async-start(), calls=%async_computation.2 | async-start | bytes 524288 | tf_op jit(solution)/shard_map/psum | solution.py:11
  510.2 326.4 %all-reduce.20.cloned.1.call-start = ((), (), s32[]{:S(2)}) async-start(), calls=%async_computation.3 | async-start | bytes 524288 | tf_op jit(solution)/shard_map/psum | solution.py:11
  663.0 1.0 copy-start.4
  726.9 274.2 %all-reduce.28.cloned.1.call-start = ((), (), s32[]{:S(2)}) async-start(), calls=%async_computation.7 | async-start | bytes 1048576 | tf_op jit(solution)/shard_map/psum | solution.py:11
  838.4 318.5 %all-reduce.22.cloned.1.call-start = ((), (), s32[]{:S(2)}) async-start(), calls=%async_computation.4 | async-start | bytes 524288 | tf_op jit(solution)/shard_map/psum | solution.py:11
  838.4 162.7 %copy-start.2 = (f32[1,256,256]{1,2,0:T(8,128)S(1)}, f32[1,256,256]{1,2,0:T(8,128)}, u32[]{:S(2)}) copy-start(f32[1,256,256]{1,2,0:T(8,128)} %all-reduce.20.cloned.1.call-done) | copy-start | bytes 786436
  1003.9 326.4 %all-reduce.24.cloned.1.call-start = ((), (), s32[]{:S(2)}) async-start(), calls=%async_computation.5 | async-start | bytes 524288 | tf_op jit(solution)/shard_map/psum | solution.py:11
  1157.9 1.0 copy-start.5
  1221.8 273.2 %all-reduce.26.cloned.1.call-start = ((), (), s32[]{:S(2)}) async-start(), calls=%async_computation.6 | async-start | bytes 1048576 | tf_op jit(solution)/shard_map/psum | solution.py:11
  1332.1 162.9 %copy-start = (f32[1,256,256]{1,2,0:T(8,128)S(1)}, f32[1,256,256]{1,2,0:T(8,128)}, u32[]{:S(2)}) copy-start(f32[1,256,256]{1,2,0:T(8,128)} %all-reduce.24.cloned.1.call-done) | copy-start | bytes 786436
Sparse Core Ops, SparseCore 0:
  10.8 159.0 all-reduce.13
  233.3 109.2 all-reduce.15
  346.5 160.8 all-reduce.29
  510.6 152.3 all-reduce.17
  727.0 109.4 all-reduce.19
  840.2 160.8 all-reduce.27
  1004.5 152.2 all-reduce.21
  1221.9 108.3 all-reduce.23
  1334.1 160.8 all-reduce.25
where the time goes:
time: 1510 us
  waiting for transfers between devices  1280 us (85%)
  other arithmetic  174 us (12%)
  local copies, waits for them, and re-layouts  18.9 us (1%)
  between operations  18.3 us (1%)
    psum x9, waiting for transfers between devices, broadcast(): return lax.psum(kept, axis)  1280 us
    another operation x20, other arithmetic, shards(): factor = jnp.linalg.cholesky(corner)  103 us
    another operation x7, other arithmetic, solve_rows(): lax.linalg.triangular_solve(factor, flat, left_side=False, lower=True, tr...  59.1 us
  transfers between devices with their start and end apart: 9, of which 9 were waited for; matrix products, arithmetic and copies ran while one was open for 0% of the time, Pallas kernels for 0%

commit v1 on v0

v1 whole, which is shorter than its diff:
```python
import functools

import jax
import jax.numpy as jnp
from jax import lax
from jax.experimental import pallas as pl
from jax.experimental.pallas import tpu as pltpu
from jax.sharding import PartitionSpec as P

F32 = jnp.float32
BF16 = jnp.bfloat16
NB = 256
TB = 128
STEPS = 6
NX, NY, NQ = 4, 8, 16
VMEM = pltpu.VMEM
MESH = pl.DeviceIdType.MESH


def exchange(x_ref, b_ref, r_ref, d_ref, s1s, s1r, s2s, s2r, s3s, s3r,
             t1s, t1r, t2s, t2r, u1s, u1r, u2s, u2r, u3s, u3r, loc):
    p = lax.axis_index("row")
    q = lax.axis_index("col")
    x = p // NY
    y = p % NY

    barrier = pltpu.get_barrier_semaphore()

    def peer(dst, src, ssem, rsem, pp, qq):
        return pltpu.make_async_remote_copy(
            src_ref=src, dst_ref=dst, send_sem=ssem, recv_sem=rsem,
            device_id=(pp, qq), device_id_type=MESH)

    def row_of(xx, yy):
        return lax.rem(xx, NX) * NY + lax.rem(yy, NY)

    for k in range(1, NX):
        pl.semaphore_signal(barrier, inc=1, device_id=(row_of(x + k, y), q), device_id_type=MESH)
    for k in range(1, NY):
        pl.semaphore_signal(barrier, inc=1, device_id=(row_of(x, y + k), q), device_id_type=MESH)
    for k in range(1, NQ):
        pl.semaphore_signal(barrier, inc=1, device_id=(p, lax.rem(q + k, NQ)), device_id_type=MESH)
    pl.semaphore_wait(barrier, NX - 1 + NY - 1 + NQ - 1)

    xs = pl.ds(pl.multiple_of(x * 64, 64), 64)
    qs = pl.ds(pl.multiple_of(q * 16, 16), 16)

    for i in range(3):
        @pl.when((x == 0) & (y == i))
        def _():
            own = pltpu.make_async_copy(x_ref.at[:, 0:64, :], b_ref.at[i, :, 0:64, :], loc.at[0])
            own.start()
            for k in range(1, NX):
                ks = pl.ds(64 * k, 64)
                peer(b_ref.at[i, :, ks, :], x_ref.at[:, ks, :], s1s.at[k - 1], s1r,
                     row_of(x + k, y), q).start()
            own.wait()
    for j in range(3):
        @pl.when(q == j)
        def _():
            own = pltpu.make_async_copy(x_ref.at[0, qs, :], r_ref.at[j, qs, :], loc.at[1])
            own.start()
            for k in range(1, NQ):
                o = lax.rem(q + k, NQ)
                os = pl.ds(pl.multiple_of(o * 16, 16), 16)
                peer(r_ref.at[j, os, :], x_ref.at[0, os, :], t1s.at[k - 1], t1r.at[j], p, o).start()
            own.wait()
    for i in range(3):
        @pl.when(y == i)
        def _():
            @pl.when(x > 0)
            def _():
                peer(b_ref.at[i, :, xs, :], b_ref.at[i, :, xs, :], s1s.at[0], s1r, p, q).wait_recv()
            for k in range(1, NY):
                peer(b_ref.at[i, :, xs, :], b_ref.at[i, :, xs, :], s2s.at[k - 1], s2r.at[i],
                     row_of(x, y + k), q).start()
    for j in range(3):
        @pl.when(q != j)
        def _():
            peer(r_ref.at[j, qs, :], r_ref.at[j, qs, :], t1s.at[0], t1r.at[j], p, q).wait_recv()
    for k in range(1, NQ):
        peer(r_ref.at[:, qs, :], r_ref.at[:, qs, :], t2s.at[k - 1], t2r.at[k - 1],
             p, lax.rem(q + k, NQ)).start()
    for i in range(3):
        @pl.when(y != i)
        def _():
            peer(b_ref.at[i, :, xs, :], b_ref.at[i, :, xs, :], s2s.at[0], s2r.at[i], p, q).wait_recv()
    for k in range(1, NX):
        peer(b_ref.at[:, :, xs, :], b_ref.at[:, :, xs, :], s3s.at[k - 1], s3r.at[k - 1],
             row_of(x + k, y), q).start()
    for k in range(1, NQ):
        o = lax.rem(q + NQ - k, NQ)
        os = pl.ds(pl.multiple_of(o * 16, 16), 16)
        peer(r_ref.at[:, qs, :], r_ref.at[:, os, :], t2s.at[k - 1], t2r.at[k - 1], p, o).wait_recv()
    for i in range(3):
        n = 3 - i
        @pl.when((x == 0) & (y == i))
        def _():
            own = pltpu.make_async_copy(r_ref.at[i:3, 0:64, :], d_ref.at[i, i:3, 0:64, :], loc.at[0])
            own.start()
            for k in range(1, NX):
                ks = pl.ds(64 * k, 64)
                peer(d_ref.at[i, i:3, ks, :], r_ref.at[i:3, ks, :], u1s.at[k - 1], u1r,
                     row_of(x + k, y), q).start()
            own.wait()
    for i in range(3):
        @pl.when(y == i)
        def _():
            @pl.when(x > 0)
            def _():
                peer(d_ref.at[i, i:3, xs, :], d_ref.at[i, i:3, xs, :], u1s.at[0], u1r, p, q).wait_recv()
            for k in range(1, NY):
                peer(d_ref.at[i, i:3, xs, :], d_ref.at[i, i:3, xs, :], u2s.at[k - 1], u2r.at[i],
                     row_of(x, y + k), q).start()
    for i in range(3):
        @pl.when(y != i)
        def _():
            peer(d_ref.at[i, i:3, xs, :], d_ref.at[i, i:3, xs, :], u2s.at[0], u2r.at[i], p, q).wait_recv()
    for k in range(1, NX):
        for i in range(3):
            peer(d_ref.at[i, i:3, xs, :], d_ref.at[i, i:3, xs, :], u3s.at[k - 1, i], u3r.at[k - 1, i],
                 row_of(x + k, y), q).start()
    for k in range(1, NX):
        ox = lax.rem(x + NX - k, NX)
        os = pl.ds(pl.multiple_of(ox * 64, 64), 64)
        peer(b_ref.at[:, :, xs, :], b_ref.at[:, :, os, :], s3s.at[k - 1], s3r.at[k - 1], p, q).wait_recv()
        for i in range(3):
            peer(d_ref.at[i, i:3, xs, :], d_ref.at[i, i:3, os, :], u3s.at[k - 1, i], u3r.at[k - 1, i],
                 p, q).wait_recv()
    for i in range(3):
        @pl.when((x == 0) & (y == i))
        def _():
            for k in range(1, NX):
                ks = pl.ds(64 * k, 64)
                peer(b_ref.at[i, :, ks, :], x_ref.at[:, ks, :], s1s.at[k - 1], s1r, p, q).wait_send()
                peer(d_ref.at[i, i:3, ks, :], r_ref.at[i:3, ks, :], u1s.at[k - 1], u1r, p, q).wait_send()

        @pl.when(y == i)
        def _():
            for k in range(1, NY):
                peer(b_ref.at[i, :, xs, :], b_ref.at[i, :, xs, :], s2s.at[k - 1], s2r.at[i], p, q).wait_send()
                peer(d_ref.at[i, i:3, xs, :], d_ref.at[i, i:3, xs, :], u2s.at[k - 1], u2r.at[i], p, q).wait_send()

        @pl.when(q == i)
        def _():
            for k in range(1, NQ):
                peer(r_ref.at[i, qs, :], x_ref.at[0, qs, :], t1s.at[k - 1], t1r.at[i], p, q).wait_send()
    for k in range(1, NQ):
        peer(r_ref.at[:, qs, :], r_ref.at[:, qs, :], t2s.at[k - 1], t2r.at[k - 1], p, q).wait_send()
    for k in range(1, NX):
        peer(b_ref.at[:, :, xs, :], b_ref.at[:, :, xs, :], s3s.at[k - 1], s3r.at[k - 1], p, q).wait_send()
        for i in range(3):
            peer(d_ref.at[i, i:3, xs, :], d_ref.at[i, i:3, xs, :], u3s.at[k - 1, i], u3r.at[k - 1, i],
                 p, q).wait_send()


def gather(x):
    dma = pltpu.SemaphoreType.DMA
    return pl.pallas_call(
        exchange,
        out_shape=(jax.ShapeDtypeStruct((3, 2, NB, NB), F32),
                   jax.ShapeDtypeStruct((3, NB, NB), F32),
                   jax.ShapeDtypeStruct((3, 3, NB, NB), F32)),
        in_specs=[pl.BlockSpec(memory_space=VMEM)],
        out_specs=[pl.BlockSpec(memory_space=VMEM)] * 3,
        scratch_shapes=[
            dma((3,)), dma(()), dma((7,)), dma((3,)), dma((3,)), dma((3,)),
            dma((15,)), dma((3,)), dma((15,)), dma((15,)),
            dma((3,)), dma(()), dma((7,)), dma((3,)), dma((3, 3)), dma((3, 3)),
            dma((2,)),
        ],
        compiler_params=pltpu.CompilerParams(
            collective_id=0, has_side_effects=True, vmem_limit_bytes=48 << 20),
        name="exchange",
    )(x)


def factor_tile(M):
    n = len(M)
    sub = lax.broadcasted_iota(jnp.int32, (8, TB), 0)
    lane = lax.broadcasted_iota(jnp.int32, (8, TB), 1)
    M = list(M)
    E = [jnp.where(lane == sub + 8 * g, 1.0, 0.0).astype(F32) for g in range(n)]
    wide = lambda v: jnp.broadcast_to(v, (8, TB))
    out_u, out_e = [], []
    for g in range(n):
        V = [{h: wide(M[h][:, 8 * g + k:8 * g + k + 1]) for h in range(g, n)} for k in range(8)]
        d = V[0][g]
        for k in range(8):
            inv = 1.0 / wide(V[k][g][k:k + 1, :])
            for j in range(k + 1, 8):
                s = wide(V[k][g][j:j + 1, :])
                V[j][g] = V[j][g] - (V[k][g] * s) * inv
                f = s * inv
                for h in range(g + 1, n):
                    V[j][h] = V[j][h] - V[k][h] * f
            if k:
                d = jnp.where(sub == k, V[k][g], d)
            mult = jnp.where(sub > k, V[k][g] * inv, 0.0)
            row_m, row_e = wide(M[g][k:k + 1, :]), wide(E[g][k:k + 1, :])
            M[g] = M[g] - mult * row_m
            E[g] = E[g] - mult * row_e
            for h in range(g + 1, n):
                c = V[k][h] * inv
                M[h] = M[h] - c * row_m
                E[h] = E[h] - c * row_e
        r = lax.rsqrt(d)
        out_u.append(M[g] * r)
        out_e.append(E[g] * r)
    return out_u, out_e


def split(a):
    hi = a.astype(BF16)
    return hi, (a - hi.astype(F32)).astype(BF16)


def left(a, axis):
    hi, lo = split(a)
    return jnp.concatenate([hi, lo, hi], axis)


def right(a, axis):
    hi, lo = split(a)
    return jnp.concatenate([hi, hi, lo], axis)


def mm(a, b):
    return jnp.dot(a, b, preferred_element_type=F32)


def mmt(a, b):
    return lax.dot_general(a, b, (((1,), (1,)), ((), ())), preferred_element_type=F32)


def solve(pos_ref, b_in, r_in, d_in, c_ref, o_ref, a_ref, b_ref, r_ref, acc_ref, inv_ref):
    p = pos_ref[0]
    q = pos_ref[1]
    for t in range(STEPS):
        i, h = divmod(t, 2)
        lo, hi = t * TB, (t + 1) * TB
        rows = slice(h * TB, h * TB + TB)
        if t == 0:
            tile = lambda g: d_in[0, 0, 8 * g:8 * g + 8, 0:TB]
        else:
            tile = lambda g: a_ref[lo + 8 * g:lo + 8 * g + 8, lo:hi]
        U, E = factor_tile([tile(g) for g in range(16)])
        for g in range(16):
            inv_ref[8 * g:8 * g + 8, :] = E[g]
        inv = inv_ref[...]
        inv_l = left(inv, 1)
        if t == 0:
            bt = jnp.concatenate([b_in[0, 0, 0:TB, :], b_in[0, 1, 0:TB, :]], 1)
            rt = r_in[0, :, 0:TB]
        else:
            bt = b_ref[lo:hi, :]
            rt = r_ref[:, lo:hi]
        ub = right(mm(inv_l, right(bt, 0)), 0)
        lt = mmt(left(rt, 1), right(inv, 1))
        r_ref[:, lo:hi] = lt
        lt_l = left(lt, 1)
        cur = c_ref[...] if t == 0 else acc_ref[...]
        acc_ref[...] = cur - mm(lt_l, ub)
        if t + 1 < STEPS:
            if t == 0:
                at = jnp.concatenate(
                    [d_in[0, 0, 0:TB, TB:], d_in[0, 1, 0:TB, :], d_in[0, 2, 0:TB, :]], 1)
            else:
                at = a_ref[lo:hi, hi:]
            ua = mm(inv_l, right(at, 0))
            ua_r = right(ua, 0)
            uat = left(ua.T, 1)
            if t == 0:
                for u in range(1, STEPS):
                    ui, uh = divmod(u, 2)
                    us = slice(uh * TB, uh * TB + TB)
                    rest = [d_in[ui, j, us, :] for j in range(ui, 3)]
                    rest[0] = rest[0][:, uh * TB:]
                    w = (STEPS - u) * TB
                    upd = mm(uat[(u - 1) * TB:u * TB, :], ua_r[:, (STEPS - 1) * TB - w:])
                    a_ref[u * TB:u * TB + TB, u * TB:] = jnp.concatenate(rest, 1) - upd
                    b_ref[u * TB:u * TB + TB, :] = jnp.concatenate(
                        [b_in[ui, 0, us, :], b_in[ui, 1, us, :]], 1) - mm(uat[(u - 1) * TB:u * TB, :], ub)
                r_ref[:, hi:] = jnp.concatenate(
                    [r_in[0, :, TB:], r_in[1], r_in[2]], 1) - mm(lt_l, ua_r)
            else:
                a_ref[hi:, hi:] = a_ref[hi:, hi:] - mm(uat, ua_r)
                b_ref[hi:, :] = b_ref[hi:, :] - mm(uat, ub)
                r_ref[:, hi:] = r_ref[:, hi:] - mm(lt_l, ua_r)
    keep = p >= 3
    o_ref[1] = jnp.where(keep, acc_ref[:, NB:], 0.0)

    @pl.when(q >= 3)
    def _():
        o_ref[0] = jnp.where(keep, acc_ref[:, :NB], 0.0)

    row = lax.broadcasted_iota(jnp.int32, (NB, NB), 0) + p * NB
    col = lax.broadcasted_iota(jnp.int32, (NB, NB), 1)
    for j in range(3):
        @pl.when(q == j)
        def _():
            o_ref[0] = jnp.where(row >= col + j * NB, r_ref[:, j * NB:(j + 1) * NB], 0.0)


def factor(pos, b, r, d, c):
    vm = pl.BlockSpec(memory_space=VMEM)
    return pl.pallas_call(
        solve,
        out_shape=jax.ShapeDtypeStruct((2, NB, NB), F32),
        in_specs=[pl.BlockSpec(memory_space=pltpu.SMEM), vm, vm, vm, vm],
        out_specs=vm,
        scratch_shapes=[
            VMEM((3 * NB, 3 * NB), F32), VMEM((3 * NB, 2 * NB), F32), VMEM((NB, 3 * NB), F32),
            VMEM((NB, 2 * NB), F32), VMEM((TB, TB), F32),
        ],
        compiler_params=pltpu.CompilerParams(vmem_limit_bytes=48 << 20),
        name="factor",
    )(pos, b, r, d, c)


def shards(kernel):
    x = kernel[0].transpose(1, 0, 2)
    pos = jnp.stack([lax.axis_index("row"), lax.axis_index("col")]).astype(jnp.int32)
    b, r, d = gather(x)
    c = jnp.concatenate([x[0], x[1]], axis=1)
    out = factor(pos, b, r, d, c)
    return out.transpose(1, 0, 2)[None]


def solution(mesh):
    spec = P(None, "row", None, "col")
    return jax.shard_map(shards, mesh=mesh, in_specs=(spec,), out_specs=spec, check_vma=False)
```

time: 1510 us -> 130 us (0.09)
  the two profiles are of different devices: /device:TPU:64 before, /device:TPU:32 now
where the time goes in v1:
time: 130 us
  Pallas kernels  123 us (95%)
  local copies, waits for them, and re-layouts  6.9 us (5%)
    pallas_call x1, Pallas kernels, gather(): pl.pallas_call(exchange, out_shape=(jax.ShapeDtypeStruct((3, 2, NB, NB),...  91.8 us
    pallas_call x1, Pallas kernels, factor(): pl.pallas_call(solve, out_shape=jax.ShapeDtypeStruct((2, NB, NB), F32), i...  31 us
    unnamed x9, local copies, waits for them, and re-layouts  5.66 us

profile of v1, /device:TPU:32, one launch (start us, length us, event | category | flops | bytes accessed | tf_op | source)
XLA Modules:
  0.0 129.9 jit_solution(7418711889947960994)
XLA Ops:
  0.0 1.1 copy.5
  1.1 0.1 pad_maximum_fusion.c_ref
  1.2 91.8 %exchange.1 = (f32[3,2,256,256]{3,2,1,0:T(8,128)S(1)}, f32[3,256,256]{2,1,0:T(8,128)S(1)}, f32[3,3,256,256]{3,2,1,0:T(8,128)S(1)}) custom-call(f32[2,256,256]{2,1,0:T(8,128)S(1)} %bitcast.15), custom_call_target="tpu_custom_call" | custom-call | tf_op jit(solution)/shard_map/exchange/pallas_call | solution.py:159
  93.0 0.0 copy-start
  93.0 1.1 copy-done
  94.1 0.0 copy-start.2
  94.2 0.9 copy-done.2
  95.0 0.1 pad_add_fusion.pos_ref
  95.1 0.0 copy-start.1
  95.1 1.4 %copy-done.1 = f32[3,2,256,256]{3,2,1,0:T(8,128)S(1)} copy-done((f32[3,2,256,256]{3,2,1,0:T(8,128)S(1)}, f32[3,2,256,256]{3,2,1,0:T(8,128)}, u32[]{:S(2)}) %copy-start.1) | copy-done | bytes 1572888
  96.5 0.0 copy-start.3
  96.5 1.1 copy-done.3
  97.7 31.0 %factor.1 = f32[2,256,256]{2,1,0:T(8,128)S(1)} custom-call(s32[2]{0:T(128)S(1)} %pad_add_fusion.pos_ref, f32[3,2,256,256]{3,2,1,0:T(8,128)S(1)} %copy-done.1, f32[3,256,256]{2,1,0:T(8,128)S(1)} %copy-done.3, f32[3,3,256,256]{3,2,1,0:T(8,128)S(1)} %get-tuple-element.10.d_in, f32[256,512]{1,0:T(8,128)S(1)} %pad_maximum_fusion.c_ref), custom_call_target="tpu_custom_call" | custom-call | tf_op jit(solution)/shard_map/factor/pallas_call | solution.py:307
  128.7 1.2 copy.3
  (1 shorter events, 0.0 us)
Async XLA Ops:
  93.0 1.2 copy-start
  94.1 0.9 copy-start.2
  95.1 1.4 %copy-start.1 = (f32[3,2,256,256]{3,2,1,0:T(8,128)S(1)}, f32[3,2,256,256]{3,2,1,0:T(8,128)}, u32[]{:S(2)}) copy-start(f32[3,2,256,256]{3,2,1,0:T(8,128)} %copy-done) | copy-start | bytes 4718596
  96.5 1.1 copy-start.3

commit v2 on v1

--- a/solution.py
+++ b/solution.py
@@ -152,27 +152,6 @@
         for i in range(3):
             peer(d_ref.at[i, i:3, xs, :], d_ref.at[i, i:3, xs, :], u3s.at[k - 1, i], u3r.at[k - 1, i],
                  p, q).wait_send()
-
-
-def gather(x):
-    dma = pltpu.SemaphoreType.DMA
-    return pl.pallas_call(
-        exchange,
-        out_shape=(jax.ShapeDtypeStruct((3, 2, NB, NB), F32),
-                   jax.ShapeDtypeStruct((3, NB, NB), F32),
-                   jax.ShapeDtypeStruct((3, 3, NB, NB), F32)),
-        in_specs=[pl.BlockSpec(memory_space=VMEM)],
-        out_specs=[pl.BlockSpec(memory_space=VMEM)] * 3,
-        scratch_shapes=[
-            dma((3,)), dma(()), dma((7,)), dma((3,)), dma((3,)), dma((3,)),
-            dma((15,)), dma((3,)), dma((15,)), dma((15,)),
-            dma((3,)), dma(()), dma((7,)), dma((3,)), dma((3, 3)), dma((3, 3)),
-            dma((2,)),
-        ],
-        compiler_params=pltpu.CompilerParams(
-            collective_id=0, has_side_effects=True, vmem_limit_bytes=48 << 20),
-        name="exchange",
-    )(x)
 
 
 def factor_tile(M):
@@ -233,9 +212,9 @@
     return lax.dot_general(a, b, (((1,), (1,)), ((), ())), preferred_element_type=F32)
 
 
-def solve(pos_ref, b_in, r_in, d_in, c_ref, o_ref, a_ref, b_ref, r_ref, acc_ref, inv_ref):
-    p = pos_ref[0]
-    q = pos_ref[1]
+def solve(b_in, r_in, d_in, c_ref, o_ref, a_ref, b_ref, r_ref, acc_ref, inv_ref):
+    p = lax.axis_index("row")
+    q = lax.axis_index("col")
     for t in range(STEPS):
         i, h = divmod(t, 2)
         lo, hi = t * TB, (t + 1) * TB
@@ -259,7 +238,7 @@
         lt = mmt(left(rt, 1), right(inv, 1))
         r_ref[:, lo:hi] = lt
         lt_l = left(lt, 1)
-        cur = c_ref[...] if t == 0 else acc_ref[...]
+        cur = jnp.concatenate([c_ref[0], c_ref[1]], 1) if t == 0 else acc_ref[...]
         acc_ref[...] = cur - mm(lt_l, ub)
         if t + 1 < STEPS:
             if t == 0:
@@ -302,29 +281,36 @@
             o_ref[0] = jnp.where(row >= col + j * NB, r_ref[:, j * NB:(j + 1) * NB], 0.0)
 
 
-def factor(pos, b, r, d, c):
+def body(x_ref, o_ref, b_in, r_in, d_in, a_ref, b_ref, r_ref, acc_ref, inv_ref, *sems):
+    exchange(x_ref, b_in, r_in, d_in, *sems)
+    solve(b_in, r_in, d_in, x_ref, o_ref, a_ref, b_ref, r_ref, acc_ref, inv_ref)
+
+
+def factor(x):
+    dma = pltpu.SemaphoreType.DMA
     vm = pl.BlockSpec(memory_space=VMEM)
     return pl.pallas_call(
-        solve,
+        body,
         out_shape=jax.ShapeDtypeStruct((2, NB, NB), F32),
-        in_specs=[pl.BlockSpec(memory_space=pltpu.SMEM), vm, vm, vm, vm],
+        in_specs=[vm],
         out_specs=vm,
         scratch_shapes=[
+            VMEM((3, 2, NB, NB), F32), VMEM((3, NB, NB), F32), VMEM((3, 3, NB, NB), F32),
             VMEM((3 * NB, 3 * NB), F32), VMEM((3 * NB, 2 * NB), F32), VMEM((NB, 3 * NB), F32),
             VMEM((NB, 2 * NB), F32), VMEM((TB, TB), F32),
+            dma((3,)), dma(()), dma((7,)), dma((3,)), dma((3,)), dma((3,)),
+            dma((15,)), dma((3,)), dma((15,)), dma((15,)),
+            dma((3,)), dma(()), dma((7,)), dma((3,)), dma((3, 3)), dma((3, 3)),
+            dma((2,)),
         ],
-        compiler_params=pltpu.CompilerParams(vmem_limit_bytes=48 << 20),
+        compiler_params=pltpu.CompilerParams(
+            collective_id=0, has_side_effects=True, vmem_limit_bytes=48 << 20),
         name="factor",
-    )(pos, b, r, d, c)
+    )(x)
 
 
 def shards(kernel):
-    x = kernel[0].transpose(1, 0, 2)
-    pos = jnp.stack([lax.axis_index("row"), lax.axis_index("col")]).astype(jnp.int32)
-    b, r, d = gather(x)
-    c = jnp.concatenate([x[0], x[1]], axis=1)
-    out = factor(pos, b, r, d, c)
-    return out.transpose(1, 0, 2)[None]
+    return factor(kernel[0].transpose(1, 0, 2)).transpose(1, 0, 2)[None]
 
 
 def solution(mesh):

time: 130 us -> 125 us (0.962)
  local copies, waits for them, and re-layouts: 6.9 us -> 2.27 us
    unnamed x9 -> x1, local copies, waits for them, and re-layouts: 5.66 us -> 1.08 us
    pallas_call x2 -> x1, Pallas kernels: 123 us -> 122 us  [factor(): pl.pallas_call(body, out_shape=jax.ShapeDtypeStruct((2, NB, NB), F32), in...]
where the time goes in v2:
time: 125 us
  Pallas kernels  122 us (98%)
  local copies, waits for them, and re-layouts  2.27 us (2%)
    pallas_call x1, Pallas kernels, factor(): pl.pallas_call(body, out_shape=jax.ShapeDtypeStruct((2, NB, NB), F32), in...  122 us

profile of v2, /device:TPU:32, one launch (start us, length us, event | category | flops | bytes accessed | tf_op | source)
XLA Modules:
  0.0 124.6 jit_solution(2825398918055683646)
XLA Ops:
  0.0 1.1 copy.5
  1.1 122.3 %factor.1 = f32[2,256,256]{2,1,0:T(8,128)S(1)} custom-call(f32[2,256,256]{2,1,0:T(8,128)S(1)} %bitcast.9), custom_call_target="tpu_custom_call" | custom-call | tf_op jit(solution)/shard_map/factor/pallas_call | solution.py:292
  123.4 1.2 copy.3

commit v3 on v0

v3 whole, which is shorter than its diff:
```python
import functools

import jax
import jax.numpy as jnp
from jax import lax
from jax.experimental import pallas as pl
from jax.experimental.pallas import tpu as pltpu
from jax.sharding import PartitionSpec as P

F32 = jnp.float32
BF16 = jnp.bfloat16
NB = 256
TB = 128
STEPS = 6
NX, NY, NZ = 4, 8, 8
TILES = (("L", 0), (0, 1), ("L", 1), (0, 2), (0, 3), (1, 2), (1, 3), ("L", 2), (2, 3),
         (0, 4), (0, 5), (1, 4), (1, 5), (2, 4), (2, 5), ("L", 3), (3, 4), (3, 5),
         ("L", 4), (4, 5), ("L", 5))
SLOT = {name: k for k, name in enumerate(TILES)}
GROUPS = ((0, 2), (2, 7), (7, 15), (15, 18), (18, 20), (20, 21))
NG = len(GROUPS)
SR = TB // 8
FAR = (4, 3, 5, 2, 6, 1, 7)
VMEM = pltpu.VMEM
MESH = pl.DeviceIdType.MESH


def remote(src, dst, ssem, rsem, dev):
    return pltpu.make_async_remote_copy(
        src_ref=src, dst_ref=dst, send_sem=ssem, recv_sem=rsem,
        device_id=dev, device_id_type=MESH)


def factor_tile(M, done):
    n = len(M)
    sub = lax.broadcasted_iota(jnp.int32, (8, TB), 0)
    lane = lax.broadcasted_iota(jnp.int32, (8, TB), 1)
    M = list(M)
    E = [jnp.where(lane == sub + 8 * g, 1.0, 0.0).astype(F32) for g in range(n)]
    wide = lambda v: jnp.broadcast_to(v, (8, TB))
    for g in range(n):
        V = [{h: wide(M[h][:, 8 * g + k:8 * g + k + 1]) for h in range(g, n)} for k in range(8)]
        d = V[0][g]
        for k in range(8):
            inv = 1.0 / wide(V[k][g][k:k + 1, :])
            for j in range(k + 1, 8):
                s = wide(V[k][g][j:j + 1, :])
                V[j][g] = V[j][g] - (V[k][g] * s) * inv
                f = s * inv
                for h in range(g + 1, n):
                    V[j][h] = V[j][h] - V[k][h] * f
            if k:
                d = jnp.where(sub == k, V[k][g], d)
            mult = jnp.where(sub > k, V[k][g] * inv, 0.0)
            row_m, row_e = wide(M[g][k:k + 1, :]), wide(E[g][k:k + 1, :])
            M[g] = M[g] - mult * row_m
            E[g] = E[g] - mult * row_e
            for h in range(g + 1, n):
                c = V[k][h] * inv
                M[h] = M[h] - c * row_m
                E[h] = E[h] - c * row_e
        r = lax.rsqrt(d)
        done(g, M[g] * r, E[g] * r)


def split(a):
    hi = a.astype(BF16)
    return hi, (a - hi.astype(F32)).astype(BF16)


def left(a, axis):
    hi, lo = split(a)
    return jnp.concatenate([hi, lo, hi], axis)


def right(a, axis):
    hi, lo = split(a)
    return jnp.concatenate([hi, hi, lo], axis)


def mm(a, b):
    return jnp.dot(a, b, preferred_element_type=F32)


def mmt(a, b):
    return lax.dot_general(a, b, (((1,), (1,)), ((), ())), preferred_element_type=F32)


def body(x_ref, o_ref, b_ref, s_ref, r_ref, d_ref, t_ref, acc_ref, u_ref,
         b1s, b1r, b2s, b2r, b3s, b3r, b4s, b4r, r1s, r1r, r2s, r2r, r3s, r3r, ds, dr,
         zs, zr, ps, pr, gs, gr, ms, mr, loc):
    p = lax.axis_index("row")
    q = lax.axis_index("col")
    x = p // NY
    y = p % NY
    z = q // 2
    c = q % 2
    mate = (p, q + 1 - 2 * c)
    first = (p == 0) & (q == 0)
    late = (p > 0) | (q > 0)

    def on_x(k):
        return (lax.rem(x + k, NX) * NY + y, q)

    def on_y(k):
        return (x * NY + lax.rem(y + k, NY), q)

    def on_z(k):
        return (p, lax.rem(z + k, NZ) * 2 + c)

    barrier = pltpu.get_barrier_semaphore()

    def greet(dev):
        pl.semaphore_signal(barrier, inc=1, device_id=dev, device_id_type=MESH)

    for k in range(1, NX):
        greet(on_x(k))
    for k in range(1, NY):
        greet(on_y(k))
    for k in range(1, 2 * NZ):
        greet((p, lax.rem(q + k, 2 * NZ)))
    def part(g, o):
        lo, hi = GROUPS[g]
        return t_ref.at[lo:hi, pl.ds(pl.multiple_of(o * SR, SR), SR), :]

    def deal(g, o):
        return remote(part(g, o), part(g, o), zs.at[g, o], zr.at[g], (0, 2 * o + 1))

    def where(s, u):
        return (s // 2, u // 2, slice((s % 2) * 2, (s % 2) * 2 + 2), slice(None), slice(None),
                slice((u % 2) * TB, (u % 2) * TB + TB))

    def get(s, u):
        return d_ref[where(s, u)].reshape(TB, TB)

    def base(t):
        def done(g, u, e):
            t_ref[SLOT["L", t], 8 * g:8 * g + 8, :] = e
            if t < 2:
                u_ref[t, 8 * g:8 * g + 8, :] = u
            if t == 5 and g % 2:
                deal(NG - 1, g // 2).start()

        tile = get(t, t)
        factor_tile([tile[8 * g:8 * g + 8, :] for g in range(16)], done)

    def reach(t, cols):
        a = jnp.concatenate([get(t, u) for u in cols], 1) if len(cols) > 1 else get(t, cols[0])
        w = mm(left(t_ref[SLOT["L", t]], 1), right(a, 0))
        for k, u in enumerate(cols):
            t_ref[SLOT[t, u]] = w[:, k * TB:(k + 1) * TB]
        wr = right(w, 0)
        for s in range(t + 1, cols[-1] + 1):
            us = [u for u in cols if u >= s]
            k0 = (us[0] - cols[0]) * TB
            upd = mm(left(t_ref[SLOT[t, s]].T, 1), wr[:, k0:])
            for k, u in enumerate(us):
                d_ref[where(s, u)] = (get(s, u) - upd[:, k * TB:(k + 1) * TB]).reshape(2, 8, 8, TB)


    corner = ((1, 1), (1, 2), (2, 2))

    @pl.when(first)
    def _():
        for dev in corner:
            greet(dev)
        d_ref[0, 0] = x_ref[0]
        base(0)
        reach(0, (1,))
        base(1)
        pl.semaphore_wait(barrier, NX - 1 + NY - 1 + 2 * NZ - 1 + 3)

    near = functools.reduce(lambda a, b: a | b, [(p == i) & (q == j) for i, j in corner])
    plain = late & jnp.logical_not(near)

    @pl.when(near)
    def _():
        greet((0, 0))
        pl.semaphore_wait(barrier, NX - 1 + NY - 1 + 2 * NZ - 1 + 1)

    @pl.when(plain)
    def _():
        pl.semaphore_wait(barrier, NX - 1 + NY - 1 + 2 * NZ - 1)

    blocks = ((0, 1), (1, 1), (0, 2), (1, 2), (2, 2))
    dcopy = {}
    for k, (i, j) in enumerate(blocks):
        dcopy[i, j] = remote(x_ref.at[0], d_ref.at[i, j], ds, dr.at[k], (0, 0))

        @pl.when((p == i) & (q == j))
        def _():
            dcopy[i, j].start()

    def b1(i, k):
        o = lax.rem(x + k, NX)
        return remote(x_ref.at[:, o], s_ref, b1s.at[k - 1], b1r, on_x(k))

    def b1_in(i):
        return remote(s_ref, s_ref, b1s.at[0], b1r, (p, q))

    def b2(i, k, dealt=True):
        o = lax.rem(y + k, NY)
        src = s_ref.at[:, o] if dealt else x_ref.at[:, 0, o]
        return remote(src, b_ref.at[i, :, x, o], b2s.at[k - 1], b2r.at[i], on_y(k))

    def b2_in(i):
        return remote(b_ref.at[i, :, x, y], b_ref.at[i, :, x, y], b2s.at[0], b2r.at[i], (p, q))

    def b3(k, along_y):
        mine = b_ref.at[:, :, x, y]
        return remote(mine, mine, b3s.at[k - 1], b3r.at[k - 1], on_y(k) if along_y else on_x(k))

    def b3_in(k, along_y):
        theirs = b_ref.at[:, :, x, lax.rem(y + NY - k, NY)] if along_y else b_ref.at[:, :, lax.rem(x + NX - k, NX), y]
        return remote(theirs, theirs, b3s.at[k - 1], b3r.at[k - 1], (p, q))

    def b4(k):
        return remote(b_ref.at[:, :, x], b_ref.at[:, :, x], b4s.at[k - 1], b4r.at[k - 1], on_x(k))

    def b4_in(k):
        theirs = b_ref.at[:, :, lax.rem(x + NX - k, NX)]
        return remote(theirs, theirs, b4s.at[k - 1], b4r.at[k - 1], (p, q))

    def ring(h, up, far):
        o = lax.rem(y + (NY - far if up else far), NY)
        if h == 4:
            blk = b_ref.at[:, 0 if up else 1, :, o]
        else:
            blk = b_ref.at[:, :, :, o]
        k = 2 * (h - 1) + (0 if up else 1)
        return remote(blk, blk, b4s.at[k], b4r.at[k], on_y(1 if up else NY - 1))

    def hop(h):
        @pl.when(c == 1)
        def _():
            for up in (True, False):
                if h > 1:
                    ring(h - 1, up, h - 1).wait_recv()
            for up in (True, False):
                ring(h, up, h - 1).start()

    def mine16(o):
        return x_ref.at[0, o // 4, pl.ds(2 * lax.rem(o, 4), 2)]

    def r1(j, k):
        o = lax.rem(q + k, 2 * NZ)
        return remote(mine16(o), r_ref.at[j, o // 2, lax.rem(o, 2)], r1s.at[k - 1], r1r.at[j], (p, o))

    def r1_in(j):
        return remote(r_ref.at[j, z, c], r_ref.at[j, z, c], r1s.at[0], r1r.at[j], (p, q))

    def r2(k):
        return remote(r_ref.at[:, z, c], r_ref.at[:, z, c], r2s.at[k - 1], r2r.at[k - 1], on_z(k))

    def r2_in(k):
        o = lax.rem(z + NZ - k, NZ)
        return remote(r_ref.at[:, z, c], r_ref.at[:, o, c], r2s.at[k - 1], r2r.at[k - 1], (p, q))

    def r3():
        return remote(r_ref.at[:, :, c], r_ref.at[:, :, c], r3s, r3r, mate)

    def r3_in():
        return remote(r_ref.at[:, :, c], r_ref.at[:, :, 1 - c], r3s, r3r, mate)

    for i in range(3):
        @pl.when((x == 0) & (y == i))
        def _():
            own = pltpu.make_async_copy(x_ref.at[:, 0, i], b_ref.at[i, :, 0, i], loc.at[0])
            own.start()
            for k in (2, 1, 3):
                b1(i, k).start()
            for k in FAR:
                b2(i, k, False).start()
            own.wait()

        @pl.when(q == i)
        def _():
            own = pltpu.make_async_copy(mine16(q), r_ref.at[i, z, c], loc.at[1])
            own.start()
            for k in range(1, 2 * NZ):
                r1(i, k).start()
            own.wait()

    def send_b2():
        for i in range(3):
            @pl.when((x > 0) & (y == i))
            def _():
                b1_in(i).wait_recv()
                own = pltpu.make_async_copy(s_ref.at[:, i], b_ref.at[i, :, x, i], loc.at[0])
                own.start()
                for k in FAR:
                    b2(i, k).start()
                own.wait()

    def send_b3():
        for i in range(3):
            @pl.when(y != i)
            def _():
                b2_in(i).wait_recv()

        @pl.when(c == 0)
        def _():
            for k in FAR:
                b3(k, True).start()

        @pl.when(c == 1)
        def _():
            for k in (2, 1, 3):
                b3(k, False).start()

    def send_b4():
        @pl.when(c == 0)
        def _():
            for k in range(1, NY):
                b3_in(k, True).wait_recv()
            for k in (2, 1, 3):
                b4(k).start()

        @pl.when(c == 1)
        def _():
            for k in range(1, NX):
                b3_in(k, False).wait_recv()
        hop(1)

    def get_b4():
        @pl.when(c == 0)
        def _():
            for k in range(1, NX):
                b4_in(k).wait_recv()

        @pl.when(c == 1)
        def _():
            for up in (True, False):
                ring(4, up, 4).wait_recv()

    def drain():
        for i in range(3):
            @pl.when(y == i)
            def _():
                for k in range(1, NY):
                    b2(i, k).wait_send()

        @pl.when(c == 0)
        def _():
            for k in range(1, NY):
                b3(k, True).wait_send()
            for k in range(1, NX):
                b4(k).wait_send()

        @pl.when(c == 1)
        def _():
            for k in range(1, NX):
                b3(k, False).wait_send()
            for h in range(1, 5):
                for up in (True, False):
                    ring(h, up, h - 1).wait_send()
        for k in range(1, NZ):
            r2(k).wait_send()
        r3().wait_send()

    def send_r2():
        for j in range(3):
            @pl.when(q != j)
            def _():
                r1_in(j).wait_recv()
        for k in FAR:
            r2(k).start()

    def send_r3():
        for k in range(1, NZ):
            r2_in(k).wait_recv()
        r3().start()

    plane = tuple((k, functools.partial(on_y, f), (x == 0) & (y == 0)) for k, f in enumerate(FAR)) + tuple(
        (7 + k, functools.partial(on_x, f), x == 0) for k, f in enumerate((2, 1, 3)))

    def spread(g, arm, dev):
        return remote(part(g, z), part(g, z), ps.at[g, arm], zr.at[g], dev)

    def pick(g, k):
        return remote(part(g, z), part(g, z), gs.at[g, k - 1], gr.at[g, k - 1], on_z(k))

    def pick_in(g, k):
        o = lax.rem(z + NZ - k, NZ)
        return remote(part(g, o), part(g, o), gs.at[g, k - 1], gr.at[g, k - 1], (p, q))

    def share(g):
        lo, hi = GROUPS[g]
        return remote(t_ref.at[lo:hi], t_ref.at[lo:hi], ms.at[g], mr.at[g], mate)

    def pass_on(g):
        @pl.when(c == 1)
        def _():
            deal(g, 0).wait_recv()
            for arm, dev, cond in plane:
                @pl.when(cond)
                def _():
                    spread(g, arm, dev()).start()
            for k in FAR:
                pick(g, k).start()

    def take(g):
        @pl.when(c == 1)
        def _():
            for k in range(1, NZ):
                pick_in(g, k).wait_recv()

            @pl.when((p > 0) | (z > 0))
            def _():
                share(g).start()

        @pl.when(c == 0)
        def _():
            share(g).wait_recv()

    @pl.when(first)
    def _():
        def emit(g):
            for o in FAR + (0,):
                deal(g, o).start()

        emit(0)
        send_r2()
        dcopy[0, 1].wait_recv()
        dcopy[1, 1].wait_recv()
        reach(0, (2, 3))
        reach(1, (2, 3))
        emit(1)
        base(2)
        reach(2, (3,))
        send_b3()
        for j in range(3):
            dcopy[j, 2].wait_recv()
        reach(0, (4, 5))
        reach(1, (4, 5))
        reach(2, (4, 5))
        emit(2)
        base(3)
        reach(3, (4, 5))
        emit(3)
        send_b4()
        base(4)
        reach(4, (5,))
        emit(4)
        base(5)
        send_r3()
        low = lax.broadcasted_iota(jnp.int32, (TB, TB), 0) >= lax.broadcasted_iota(jnp.int32, (TB, TB), 1)
        o_ref[0, 0:TB, 0:TB] = jnp.where(low, u_ref[0].T, 0.0)
        o_ref[0, 0:TB, TB:] = jnp.zeros((TB, TB), F32)
        o_ref[0, TB:, 0:TB] = t_ref[SLOT[0, 1]].T
        o_ref[0, TB:, TB:] = jnp.where(low, u_ref[1].T, 0.0)
        o_ref[1] = jnp.zeros((NB, NB), F32)
        r3_in().wait_recv()
        get_b4()
        drain()
        for g in range(NG):
            for o in range(NZ):
                deal(g, o).wait_send()

    @pl.when(late)
    def _():
        def rcols(s):
            return (s // 2, slice(None), slice(None), slice(None), slice(None), slice((s % 2) * TB, (s % 2) * TB + TB))

        def brow(s):
            return [(s // 2, j, slice((s % 2) * 2, (s % 2) * 2 + 2)) for j in range(2)]

        def apply(t):
            inv = t_ref[SLOT["L", t]]
            bt = jnp.concatenate([b_ref[k].reshape(TB, NB) for k in brow(t)], 1)
            ub = right(mm(left(inv, 1), right(bt, 0)), 0)
            lt = mmt(left(r_ref[rcols(t)].reshape(NB, TB), 1), right(inv, 1))
            r_ref[rcols(t)] = lt.reshape(NZ, 2, 2, 8, TB)
            lt = left(lt, 1)
            cur = jnp.concatenate([x_ref[0].reshape(NB, NB), x_ref[1].reshape(NB, NB)], 1) if t == 0 else acc_ref[...]
            acc_ref[...] = cur - mm(lt, ub)
            for s in range(t + 1, STEPS):
                u = t_ref[SLOT[t, s]]
                upd = mm(left(u.T, 1), ub)
                for j, k in enumerate(brow(s)):
                    b_ref[k] = b_ref[k] - upd[:, j * NB:(j + 1) * NB].reshape(2, 8, 8, NB)
                r_ref[rcols(s)] = r_ref[rcols(s)] - mm(lt, right(u, 0)).reshape(NZ, 2, 2, 8, TB)

        send_b2()
        send_r2()
        send_b3()
        pass_on(0)
        send_r3()
        send_b4()
        pass_on(1)
        hop(2)
        take(0)
        pass_on(2)
        hop(3)
        take(1)
        r3_in().wait_recv()
        pass_on(3)
        hop(4)
        take(2)
        pass_on(4)
        take(3)
        pass_on(5)
        get_b4()
        drain()
        take(4)
        for t in range(5):
            apply(t)
        take(5)
        apply(5)
        keep = p >= 3
        o_ref[1] = jnp.where(keep, acc_ref[:, NB:], 0.0)

        @pl.when(q >= 3)
        def _():
            o_ref[0] = jnp.where(keep, acc_ref[:, :NB], 0.0)

        row = lax.broadcasted_iota(jnp.int32, (NB, NB), 0) + p * NB
        col = lax.broadcasted_iota(jnp.int32, (NB, NB), 1)
        for j in range(3):
            @pl.when(q == j)
            def _():
                o_ref[0] = jnp.where(row >= col + j * NB, r_ref[j].reshape(NB, NB), 0.0)

        for i, j in blocks:
            @pl.when((p == i) & (q == j))
            def _():
                dcopy[i, j].wait_send()

        @pl.when(c == 1)
        def _():
            for g in range(NG):
                for k in range(1, NZ):
                    pick(g, k).wait_send()
            for arm, dev, cond in plane:
                @pl.when(cond)
                def _():
                    for g in range(NG):
                        spread(g, arm, dev()).wait_send()

            @pl.when((p > 0) | (z > 0))
            def _():
                for g in range(NG):
                    share(g).wait_send()

    for i in range(3):
        @pl.when((x == 0) & (y == i))
        def _():
            for k in range(1, NX):
                b1(i, k).wait_send()

        @pl.when(q == i)
        def _():
            for k in range(1, 2 * NZ):
                r1(i, k).wait_send()


def factor(x):
    dma = pltpu.SemaphoreType.DMA
    vm = pl.BlockSpec(memory_space=VMEM)
    return pl.pallas_call(
        body,
        out_shape=jax.ShapeDtypeStruct((2, NB, NB), F32),
        in_specs=[vm],
        out_specs=vm,
        scratch_shapes=[
            VMEM((3, 2, NX, NY, 8, NB), F32), VMEM((2, NY, 8, NB), F32), VMEM((3, NZ, 2, 2, 8, NB), F32), VMEM((3, 3, NX, NY, 8, NB), F32),
            VMEM((len(TILES), TB, TB), F32), VMEM((NB, 2 * NB), F32), VMEM((2, TB, TB), F32),
            dma((3,)), dma(()), dma((7,)), dma((3,)), dma((7,)), dma((7,)), dma((8,)), dma((8,)),
            dma((15,)), dma((3,)), dma((7,)), dma((7,)), dma(()), dma(()), dma(()), dma((5,)),
            dma((NG, 8)), dma((NG,)), dma((NG, 10)), dma((NG,)), dma((NG, 7)), dma((NG, 7)), dma((NG,)), dma((NG,)),
            dma((2,)),
        ],
        compiler_params=pltpu.CompilerParams(
            collective_id=0, has_side_effects=True, vmem_limit_bytes=48 << 20),
        name="factor",
    )(x)


def shards(kernel):
    x = kernel[0].transpose(1, 0, 2).reshape(2, NX, NY, 8, NB)
    return factor(x).transpose(1, 0, 2)[None]


def solution(mesh):
    spec = P(None, "row", None, "col")
    return jax.shard_map(shards, mesh=mesh, in_specs=(spec,), out_specs=spec, check_vma=False)
```

time: 1510 us -> 77.7 us (0.05)
  the two profiles are of different devices: /device:TPU:64 before, /device:TPU:10 now
where the time goes in v3:
time: 77.7 us; the launch traced here: 77.5 us
  Pallas kernels  75.2 us (97%)
  local copies, waits for them, and re-layouts  2.27 us (3%)
    pallas_call x1, Pallas kernels, factor(): pl.pallas_call(body, out_shape=jax.ShapeDtypeStruct((2, NB, NB), F32), in...  75.2 us

profile of v3, /device:TPU:10, one launch (start us, length us, event | category | flops | bytes accessed | tf_op | source)
XLA Modules:
  0.0 77.5 jit_solution(431731790225028405)
XLA Ops:
  0.0 1.1 %copy.2 = f32[2,256,256]{2,1,0:T(8,128)S(1)} copy(f32[2,256,256]{2,0,1:T(2,128)} %bitcast.9) | data formatting | bytes 1048576 | tf_op jit(solution)/shard_map/transpose | solution.py:580
  1.1 75.2 %factor.1 = f32[2,256,256]{2,1,0:T(8,128)S(1)} custom-call(f32[2,4,8,8,256]{4,3,2,1,0:T(8,128)S(1)} %bitcast.8), custom_call_target="tpu_custom_call" | custom-call | tf_op jit(solution)/shard_map/factor/pallas_call | solution.py:560
  76.3 1.2 %copy.3 = f32[1,256,2,256]{3,2,1,0:T(2,128)} copy(f32[1,256,2,256]{3,1,2,0:T(8,128)S(1)} %bitcast.7) | data formatting | bytes 1048576 | tf_op jit(solution)/shard_map/broadcast_in_dim | solution.py:581

commit v4 on v3

--- a/solution.py
+++ b/solution.py
@@ -273,7 +273,7 @@
                 b2(i, k, False).start()
             own.wait()
 
-        @pl.when(q == i)
+        @pl.when((q == i) & (p > 0))
         def _():
             own = pltpu.make_async_copy(mine16(q), r_ref.at[i, z, c], loc.at[1])
             own.start()
@@ -354,22 +354,39 @@
             for h in range(1, 5):
                 for up in (True, False):
                     ring(h, up, h - 1).wait_send()
-        for k in range(1, NZ):
-            r2(k).wait_send()
-        r3().wait_send()
+
+        @pl.when(p > 0)
+        def _():
+            for k in range(1, NZ):
+                r2(k).wait_send()
+            r3().wait_send()
 
     def send_r2():
         for j in range(3):
-            @pl.when(q != j)
+            @pl.when((q != j) & (p > 0))
             def _():
                 r1_in(j).wait_recv()
-        for k in FAR:
-            r2(k).start()
+
+        @pl.when(p > 0)
+        def _():
+            for k in FAR:
+                r2(k).start()
 
     def send_r3():
-        for k in range(1, NZ):
-            r2_in(k).wait_recv()
-        r3().start()
+        @pl.when(p > 0)
+        def _():
+            for k in range(1, NZ):
+                r2_in(k).wait_recv()
+            r3().start()
+
+    def get_r3():
+        @pl.when(p > 0)
+        def _():
+            r3_in().wait_recv()
+
+        @pl.when(p == 0)
+        def _():
+            r_ref[...] = jnp.zeros((3, NZ, 2, 2, 8, NB), F32)
 
     plane = tuple((k, functools.partial(on_y, f), (x == 0) & (y == 0)) for k, f in enumerate(FAR)) + tuple(
         (7 + k, functools.partial(on_x, f), x == 0) for k, f in enumerate((2, 1, 3)))
@@ -420,7 +437,6 @@
                 deal(g, o).start()
 
         emit(0)
-        send_r2()
         dcopy[0, 1].wait_recv()
         dcopy[1, 1].wait_recv()
         reach(0, (2, 3))
@@ -443,14 +459,12 @@
         reach(4, (5,))
         emit(4)
         base(5)
-        send_r3()
         low = lax.broadcasted_iota(jnp.int32, (TB, TB), 0) >= lax.broadcasted_iota(jnp.int32, (TB, TB), 1)
         o_ref[0, 0:TB, 0:TB] = jnp.where(low, u_ref[0].T, 0.0)
         o_ref[0, 0:TB, TB:] = jnp.zeros((TB, TB), F32)
         o_ref[0, TB:, 0:TB] = t_ref[SLOT[0, 1]].T
         o_ref[0, TB:, TB:] = jnp.where(low, u_ref[1].T, 0.0)
         o_ref[1] = jnp.zeros((NB, NB), F32)
-        r3_in().wait_recv()
         get_b4()
         drain()
         for g in range(NG):
@@ -485,21 +499,21 @@
         send_r2()
         send_b3()
         pass_on(0)
-        send_r3()
         send_b4()
         pass_on(1)
         hop(2)
-        take(0)
         pass_on(2)
         hop(3)
+        take(0)
         take(1)
-        r3_in().wait_recv()
+        hop(4)
         pass_on(3)
-        hop(4)
         take(2)
+        send_r3()
         pass_on(4)
         take(3)
         pass_on(5)
+        get_r3()
         get_b4()
         drain()
         take(4)
@@ -548,7 +562,7 @@
             for k in range(1, NX):
                 b1(i, k).wait_send()
 
-        @pl.when(q == i)
+        @pl.when((q == i) & (p > 0))
         def _():
             for k in range(1, 2 * NZ):
                 r1(i, k).wait_send()

time: 77.7 us -> 64 us (0.82)
  Pallas kernels: 75.2 us -> 61.5 us
    pallas_call x1, Pallas kernels: 75.2 us -> 61.5 us  [factor(): pl.pallas_call(body, out_shape=jax.ShapeDtypeStruct((2, NB, NB), F32), in...]
where the time goes in v4:
time: 64 us; the launch traced here: 63.8 us
  Pallas kernels  61.5 us (96%)
  local copies, waits for them, and re-layouts  2.27 us (4%)
    pallas_call x1, Pallas kernels, factor(): pl.pallas_call(body, out_shape=jax.ShapeDtypeStruct((2, NB, NB), F32), in...  61.5 us

profile of v4, /device:TPU:10, one launch (start us, length us, event | category | flops | bytes accessed | tf_op | source)
XLA Modules:
  0.0 63.8 jit_solution(1797799974258372915)
XLA Ops:
  0.0 1.1 %copy.2 = f32[2,256,256]{2,1,0:T(8,128)S(1)} copy(f32[2,256,256]{2,0,1:T(2,128)} %bitcast.9) | data formatting | bytes 1048576 | tf_op jit(solution)/shard_map/transpose | solution.py:594
  1.1 61.5 %factor.1 = f32[2,256,256]{2,1,0:T(8,128)S(1)} custom-call(f32[2,4,8,8,256]{4,3,2,1,0:T(8,128)S(1)} %bitcast.8), custom_call_target="tpu_custom_call" | custom-call | tf_op jit(solution)/shard_map/factor/pallas_call | solution.py:574
  62.6 1.2 %copy.3 = f32[1,256,2,256]{3,2,1,0:T(2,128)} copy(f32[1,256,2,256]{3,1,2,0:T(8,128)S(1)} %bitcast.7) | data formatting | bytes 1048576 | tf_op jit(solution)/shard_map/broadcast_in_dim | solution.py:595

commit v5 on v4

--- a/solution.py
+++ b/solution.py
@@ -516,9 +516,10 @@
         get_r3()
         get_b4()
         drain()
+        for t in range(4):
+            apply(t)
         take(4)
-        for t in range(5):
-            apply(t)
+        apply(4)
         take(5)
         apply(5)
         keep = p >= 3

time: 64 us -> 63.9 us (level)
  no operation moved by 1% of the time
where the time goes in v5:
time: 63.9 us; the launch traced here: 63.7 us
  Pallas kernels  61.4 us (96%)
  local copies, waits for them, and re-layouts  2.27 us (4%)
    pallas_call x1, Pallas kernels, factor(): pl.pallas_call(body, out_shape=jax.ShapeDtypeStruct((2, NB, NB), F32), in...  61.4 us

profile of v5, /device:TPU:10, one launch (start us, length us, event | category | flops | bytes accessed | tf_op | source)
XLA Modules:
  0.0 63.7 jit_solution(3558233846703685073)
XLA Ops:
  0.0 1.1 %copy.2 = f32[2,256,256]{2,1,0:T(8,128)S(1)} copy(f32[2,256,256]{2,0,1:T(2,128)} %bitcast.9) | data formatting | bytes 1048576 | tf_op jit(solution)/shard_map/transpose | solution.py:595
  1.1 61.4 %factor.1 = f32[2,256,256]{2,1,0:T(8,128)S(1)} custom-call(f32[2,4,8,8,256]{4,3,2,1,0:T(8,128)S(1)} %bitcast.8), custom_call_target="tpu_custom_call" | custom-call | tf_op jit(solution)/shard_map/factor/pallas_call | solution.py:575
  62.5 1.2 %copy.3 = f32[1,256,2,256]{3,2,1,0:T(2,128)} copy(f32[1,256,2,256]{3,1,2,0:T(8,128)S(1)} %bitcast.7) | data formatting | bytes 1048576 | tf_op jit(solution)/shard_map/broadcast_in_dim | solution.py:596
